TPU v7x, 512 devices: a whole 4x4x16 slice. The times are simulated.
512 devices in a mesh: ctx: 16 (over y, z_hi), exp: 16 (over x, z_lo), dp: 2 (over core).
Axes of the slice: x: 4, y: 4, z: 16 (z_hi: 4, z_lo: 4; z = z_hi * 4 + z_lo), core: 2. Of those that a mesh axis runs over, the one named last changes fastest.
Arguments:
- queries: bfloat16 [32, 3072, 2048], P(('dp', 'exp'), 'ctx'), parts along dimension 0, may hold values from -38 to 38
- keys: bfloat16 [32, 3072, 256], P(('dp', 'exp'), 'ctx'), parts along dimension 0, may hold values from -4 to 4
- values: bfloat16 [32, 3072, 256], P(('dp', 'exp'), 'ctx'), parts along dimension 0, may hold values from -6 to 6
- segments: int32 [32, 3072], P(('dp', 'exp')), parts along dimension 0, may hold values from 0 to 7, never falling along the last dimension, each value on 1 to 1536 neighbouring positions
- residual: bfloat16 [32, 3072, 1024], P(('dp', 'exp'), 'ctx'), parts along dimension 0, may hold values from -3 to 3
- out_weight: bfloat16 [2048, 1024], P('ctx'), may hold values from -0.125 to 0.125
- gain: float32 [1024], replicated, may hold values from 0.1 to 1.9
- expert_ids: int32 [32, 3072, 8], P(('dp', 'exp'), 'ctx'), parts along dimension 0, may hold values from 0 to 127, all different within a row; in each aligned block of 192 rows (0 to 191, 192 to 383, ..., all dimensions but the last counted through in order) at most 24 rows name the same one
- route_weights: float32 [32, 3072, 8], P(('dp', 'exp'), 'ctx'), parts along dimension 0, may hold values from 0.05 to 0.5
- w_gate: bfloat16 [16, 1024, 384], P('exp'), may hold values from -0.1875 to 0.1875
- w_up: bfloat16 [16, 1024, 384], P('exp'), may hold values from -0.1875 to 0.1875
- w_down: bfloat16 [16, 384, 1024], P('exp'), may hold values from -0.3125 to 0.3125
Outputs:
- layer_out: bfloat16 [32, 3072, 1024], P(('dp', 'exp'), 'ctx'), parts along dimension 0
There are 2 independent parts, one for each index of `dp`. A program takes and returns all parts, laid end to end along the dimension named above; an argument that names none is the same for every part. Nothing has to cross between parts.
Inputs may be any that keep to these rules, and one draw needn't show every extreme that they name: `expert_ids`: in every aligned block of 192 positions of a sequence (one slab), no expert is named by more than 24 tokens, and in every draw some expert is named by exactly 24 tokens of some block; a token names 8 different experts. `segments`: document numbers never fall along a sequence.
All inputs are finite; a program needn't handle non-finite values.
Results may differ from a plain program's by a relative error of at most 0.006.
Values may be sent and summed in bfloat16 or wider, within the bound.
A program may use at most 64 MiB of HBM per device.

v0:
```python
import math
import jax
import jax.numpy as jnp
from jax import lax
from jax.sharding import PartitionSpec as P

HQ = 16
KVH = 2
HD = 128
TOP = 8
CAP = 24


def per_device(
    queries,
    keys,
    values,
    segments,
    residual,
    out_weight,
    gain,
    expert_ids,
    route_weights,
    w_gate,
    w_up,
    w_down,
):
    tok_rows = queries.shape[1]
    model_width = residual.shape[2]
    groups = HQ // KVH
    scale_factor = 1.0 / math.sqrt(HD)
    rank_ctx = lax.axis_index("ctx")
    query_pos = rank_ctx * tok_rows + jnp.arange(tok_rows, dtype=jnp.int32)
    seg_line = segments[0]
    query_seg = lax.dynamic_slice_in_dim(seg_line, rank_ctx * tok_rows, tok_rows)
    query_heads = queries[0].reshape(tok_rows, KVH, groups, HD)

    def attend_block(running, inputs):
        key_blk, value_blk, blk_start = inputs
        blk_rows = key_blk.shape[0]
        key_pos = blk_start + jnp.arange(blk_rows, dtype=jnp.int32)
        key_seg = lax.dynamic_slice_in_dim(seg_line, blk_start, blk_rows)
        run_max, run_sum, accum = running
        scores = (
            jnp.einsum("qkgd,skd->qkgs", query_heads, key_blk, preferred_element_type=jnp.float32)
            * scale_factor
        )
        allowed = (
            (key_pos[None, :] <= query_pos[:, None]) & (key_seg[None, :] == query_seg[:, None])
        )[:, None, None, :]
        masked_scores = jnp.where(allowed, scores, -1e30)
        new_max = jnp.maximum(run_max, jnp.max(masked_scores, axis=-1))
        correction = jnp.exp(run_max - new_max)
        expo = jnp.where(allowed, jnp.exp(scores - new_max[..., None]), 0.0)
        new_sum = run_sum * correction + jnp.sum(expo, axis=-1)
        probs = expo.astype(jnp.bfloat16)
        new_accum = accum * correction[..., None] + jnp.einsum(
            "qkgs,skd->qkgd", probs, value_blk, preferred_element_type=jnp.float32
        )
        updated = (new_max, new_sum, new_accum)
        return (updated, None)

    initial = (
        jnp.full((tok_rows, KVH, groups), -1e30, jnp.float32),
        jnp.zeros((tok_rows, KVH, groups), jnp.float32),
        jnp.zeros((tok_rows, KVH, groups, HD), jnp.float32),
    )
    running = initial
    key_piece = lax.all_gather(keys, "ctx", axis=1, tiled=True)
    value_piece = lax.all_gather(values, "ctx", axis=1, tiled=True)
    row_count = key_piece.shape[1]
    blk_rows = math.gcd(row_count, 512)
    blk_count = row_count // blk_rows
    key_blocks = key_piece[0].reshape(blk_count, blk_rows, KVH, HD)
    value_blocks = value_piece[0].reshape(blk_count, blk_rows, KVH, HD)
    blk_starts = blk_rows * jnp.arange(blk_count, dtype=jnp.int32)
    running, _ = lax.scan(attend_block, running, (key_blocks, value_blocks, blk_starts))
    run_max, run_sum, accum = running
    attended = (accum / run_sum[..., None]).reshape(tok_rows, HQ * HD).astype(jnp.bfloat16)
    projected = jnp.dot(
        attended,
        lax.all_gather(out_weight, "ctx", axis=0, tiled=True),
        preferred_element_type=jnp.float32,
    )
    hidden_state = residual[0].astype(jnp.float32) + projected
    normed = (
        hidden_state
        * lax.rsqrt(jnp.mean(hidden_state * hidden_state, axis=-1, keepdims=True) + 1e-06)
        * gain
    ).astype(jnp.bfloat16)
    owners = lax.axis_size("exp")
    chosen = expert_ids[0]
    active = chosen < owners
    owner_range = jnp.arange(owners, dtype=jnp.int32)
    hit_table = (
        ((chosen[:, :, None] == owner_range) & active[:, :, None])
        .astype(jnp.int32)
        .reshape(tok_rows * TOP, owners)
    )
    rank_in = jnp.sum((jnp.cumsum(hit_table, axis=0) - 1) * hit_table, axis=1).reshape(
        tok_rows, TOP
    )
    slot_total = owners * CAP
    slot_of = jnp.where(active, chosen * CAP + rank_in, slot_total)
    slot_range = jnp.arange(slot_total, dtype=jnp.int32)
    placing = jnp.any(slot_of[None, :, :] == slot_range[:, None, None], axis=2).astype(jnp.bfloat16)
    outgoing = (
        jnp.dot(placing, normed, preferred_element_type=jnp.float32)
        .astype(jnp.bfloat16)
        .reshape(owners, CAP, model_width)
    )
    arrived = lax.all_to_all(outgoing, "exp", split_axis=0, concat_axis=0, tiled=True)
    item_count = arrived.shape[1]
    flat_rows = arrived.reshape(owners * item_count, model_width)
    gate_part = jnp.dot(flat_rows, w_gate[0], preferred_element_type=jnp.float32)
    up_part = jnp.dot(flat_rows, w_up[0], preferred_element_type=jnp.float32)
    expert_hidden = (jax.nn.silu(gate_part) * up_part).astype(jnp.bfloat16)
    expert_out = jnp.dot(expert_hidden, w_down[0], preferred_element_type=jnp.float32).astype(
        jnp.bfloat16
    )
    returned = lax.all_to_all(
        expert_out.reshape(owners, item_count, model_width),
        "exp",
        split_axis=0,
        concat_axis=0,
        tiled=True,
    )
    padded_back = jnp.concatenate(
        [returned.reshape(slot_total, model_width), jnp.zeros((1, model_width), jnp.bfloat16)],
        axis=0,
    )
    picked = padded_back[slot_of]
    mix_weights = jnp.where(active, route_weights[0], 0.0)
    moe_sum = jnp.einsum("tk,tkd->td", mix_weights, picked.astype(jnp.float32))
    layer_out = (hidden_state + moe_sum).astype(jnp.bfloat16)
    return layer_out[None]


def solution(mesh):
    return jax.shard_map(
        per_device,
        mesh=mesh,
        in_specs=(
            P(("dp", "exp"), "ctx", None),
            P(("dp", "exp"), "ctx", None),
            P(("dp", "exp"), "ctx", None),
            P(("dp", "exp"), None),
            P(("dp", "exp"), "ctx", None),
            P("ctx", None),
            P(),
            P(("dp", "exp"), "ctx", None),
            P(("dp", "exp"), "ctx", None),
            P("exp", None, None),
            P("exp", None, None),
            P("exp", None, None),
        ),
        out_specs=P(("dp", "exp"), "ctx", None),
        check_vma=False,
    )
```

profile of v0, /device:TPU:1, one launch (start us, length us, event | category | flops | bytes accessed | tf_op | source)
XLA Modules:
  0.0 393.0 jit_solution(8537777085268056994)
XLA Ops:
  10.4 4.5 %reduce-window.6 = s32[16,12,128]{2,1,0:T(8,128)S(1)} reduce-window(s32[16,12,128]{2,1,0:T(8,128)S(1)} %fusion.41, s32[]{:T(128)} %constant.11.clone.1), window={size=1x1x128 pad=0_0x0_0x127_0}, to_apply=%region_4.5 | reduce-window | flops 3121152 | bytes 196612 | tf_op jit(solution)/shard_map/reduce-window
  20.8 79.8 %all-gather.6.cloned.1.call-done = bf16[1,3072,256]{2,1,0:T(8,128)(2,1)} async-done(((bf16[1,192,256]{2,1,0:T(8,128)(2,1)}), bf16[1,3072,256]{2,1,0:T(8,128)(2,1)}) %all-gather.6.cloned.1.call-update) | async-done | bytes 1572880 | tf_op jit(solution)/shard_map/all_gather | solution.py:70
  103.0 81.9 %all-gather.4.cloned.1.call-done = bf16[1,3072,256]{2,1,0:T(8,128)(2,1)} async-done(((bf16[1,192,256]{2,1,0:T(8,128)(2,1)}), bf16[1,3072,256]{2,1,0:T(8,128)(2,1)}) %all-gather.4.cloned.1.call-update) | async-done | bytes 1572880 | tf_op jit(solution)/shard_map/all_gather | solution.py:69
  188.3 116.4 %while.15 = (s32[]{:T(128)}, f32[192,2,8]{0,2,1:T(8,128)S(1)}, f32[192,2,8]{0,2,1:T(8,128)S(1)}, f32[192,2,8,128]{3,0,2,1:T(8,128)}, s32[6]{0:T(128)}, /*index=5...) while((s32[]{:T(128)}, f32[192,2,8]{0,2,1:T(8,128)S(1)}, ...), condition=%wide.region_3.4_spmd.clone, body=%wide.region_0.3_spmd.clone.sunk | while | flops 824098496 | bytes 50147816 | solution.py:77
  198.7 4.3 %fusion.61 = f32[192,2,8]{0,2,1:T(8,128)S(1)} fusion(f32[2,512,192,8]{1,2,3,0:T(8,128)} %get-tuple-element.231, f32[192,2,8]{0,2,1:T(8,128)S(1)} %select_maximum_fusion.2, pred[192,512]{1,0:T(8,128)(4,1)S(1)} %compare_and_fusion.2), kind=kLoop, calls=%fused_computation.8.clone.1 | loop fusion | flops 6288384 | bytes 6414336 | tf_op jit(solution)/shard_map/while/body/eval_jaxpr/reduce_sum | solution.py:55
  213.3 3.7 fusion.60
  217.1 4.3 %fusion.61 = f32[192,2,8]{0,2,1:T(8,128)S(1)} fusion(f32[2,512,192,8]{1,2,3,0:T(8,128)} %get-tuple-element.231, f32[192,2,8]{0,2,1:T(8,128)S(1)} %select_maximum_fusion.2, pred[192,512]{1,0:T(8,128)(4,1)S(1)} %compare_and_fusion.2), kind=kLoop, calls=%fused_computation.8.clone.1 | loop fusion | flops 6288384 | bytes 6414336 | tf_op jit(solution)/shard_map/while/body/eval_jaxpr/reduce_sum | solution.py:55
  221.7 4.5 %bitcast_add_fusion.4 = f32[192,2,8,128]{3,0,2,1:T(8,128)} fusion(f32[192,2,8,128]{3,0,2,1:T(8,128)} %get-tuple-element.252, f32[2,512,192,8]{1,2,3,0:T(8,128)S(1)} %copy-done.1, f32[192,2,8]{0,2,1:T(8,128)S(1)} %select_maximum_fusion.2, pred[192,512]{1,0:T(8,128)(4,1)S(1)} %compare_and_fusion.2, f32[192,2,8]{0,2,1:T(8,128)S(1)} %get-tuple-element.233, ...), kind=kOutput, calls=%fused_computation.14.clone.1 | convolution fusion | flops 410124288 | bytes 9822209 | tf_op jit(solution)/shard_map/while/body/eval_jaxpr/qkgs,skd->qkgd/dot_general | solution.py:57
  232.9 3.7 fusion.60
  236.7 4.3 %fusion.61 = f32[192,2,8]{0,2,1:T(8,128)S(1)} fusion(f32[2,512,192,8]{1,2,3,0:T(8,128)} %get-tuple-element.231, f32[192,2,8]{0,2,1:T(8,128)S(1)} %select_maximum_fusion.2, pred[192,512]{1,0:T(8,128)(4,1)S(1)} %compare_and_fusion.2), kind=kLoop, calls=%fused_computation.8.clone.1 | loop fusion | flops 6288384 | bytes 6414336 | tf_op jit(solution)/shard_map/while/body/eval_jaxpr/reduce_sum | solution.py:55
  241.3 4.7 %bitcast_add_fusion.4 = f32[192,2,8,128]{3,0,2,1:T(8,128)} fusion(f32[192,2,8,128]{3,0,2,1:T(8,128)} %get-tuple-element.252, f32[2,512,192,8]{1,2,3,0:T(8,128)S(1)} %copy-done.1, f32[192,2,8]{0,2,1:T(8,128)S(1)} %select_maximum_fusion.2, pred[192,512]{1,0:T(8,128)(4,1)S(1)} %compare_and_fusion.2, f32[192,2,8]{0,2,1:T(8,128)S(1)} %get-tuple-element.233, ...), kind=kOutput, calls=%fused_computation.14.clone.1 | convolution fusion | flops 410124288 | bytes 9822209 | tf_op jit(solution)/shard_map/while/body/eval_jaxpr/qkgs,skd->qkgd/dot_general | solution.py:57
  252.6 3.7 fusion.60
  256.4 4.3 %fusion.61 = f32[192,2,8]{0,2,1:T(8,128)S(1)} fusion(f32[2,512,192,8]{1,2,3,0:T(8,128)} %get-tuple-element.231, f32[192,2,8]{0,2,1:T(8,128)S(1)} %select_maximum_fusion.2, pred[192,512]{1,0:T(8,128)(4,1)S(1)} %compare_and_fusion.2), kind=kLoop, calls=%fused_computation.8.clone.1 | loop fusion | flops 6288384 | bytes 6414336 | tf_op jit(solution)/shard_map/while/body/eval_jaxpr/reduce_sum | solution.py:55
  261.0 4.5 %bitcast_add_fusion.4 = f32[192,2,8,128]{3,0,2,1:T(8,128)} fusion(f32[192,2,8,128]{3,0,2,1:T(8,128)} %get-tuple-element.252, f32[2,512,192,8]{1,2,3,0:T(8,128)S(1)} %copy-done.1, f32[192,2,8]{0,2,1:T(8,128)S(1)} %select_maximum_fusion.2, pred[192,512]{1,0:T(8,128)(4,1)S(1)} %compare_and_fusion.2, f32[192,2,8]{0,2,1:T(8,128)S(1)} %get-tuple-element.233, ...), kind=kOutput, calls=%fused_computation.14.clone.1 | convolution fusion | flops 410124288 | bytes 9822209 | tf_op jit(solution)/shard_map/while/body/eval_jaxpr/qkgs,skd->qkgd/dot_general | solution.py:57
  272.2 3.7 fusion.60
  275.9 4.3 %fusion.61 = f32[192,2,8]{0,2,1:T(8,128)S(1)} fusion(f32[2,512,192,8]{1,2,3,0:T(8,128)} %get-tuple-element.231, f32[192,2,8]{0,2,1:T(8,128)S(1)} %select_maximum_fusion.2, pred[192,512]{1,0:T(8,128)(4,1)S(1)} %compare_and_fusion.2), kind=kLoop, calls=%fused_computation.8.clone.1 | loop fusion | flops 6288384 | bytes 6414336 | tf_op jit(solution)/shard_map/while/body/eval_jaxpr/reduce_sum | solution.py:55
  280.7 4.5 %bitcast_add_fusion.4 = f32[192,2,8,128]{3,0,2,1:T(8,128)} fusion(f32[192,2,8,128]{3,0,2,1:T(8,128)} %get-tuple-element.252, f32[2,512,192,8]{1,2,3,0:T(8,128)S(1)} %copy-done.1, f32[192,2,8]{0,2,1:T(8,128)S(1)} %select_maximum_fusion.2, pred[192,512]{1,0:T(8,128)(4,1)S(1)} %compare_and_fusion.2, f32[192,2,8]{0,2,1:T(8,128)S(1)} %get-tuple-element.233, ...), kind=kOutput, calls=%fused_computation.14.clone.1 | convolution fusion | flops 410124288 | bytes 9822209 | tf_op jit(solution)/shard_map/while/body/eval_jaxpr/qkgs,skd->qkgd/dot_general | solution.py:57
  291.8 3.7 fusion.60
  295.6 4.3 %fusion.61 = f32[192,2,8]{0,2,1:T(8,128)S(1)} fusion(f32[2,512,192,8]{1,2,3,0:T(8,128)} %get-tuple-element.231, f32[192,2,8]{0,2,1:T(8,128)S(1)} %select_maximum_fusion.2, pred[192,512]{1,0:T(8,128)(4,1)S(1)} %compare_and_fusion.2), kind=kLoop, calls=%fused_computation.8.clone.1 | loop fusion | flops 6288384 | bytes 6414336 | tf_op jit(solution)/shard_map/while/body/eval_jaxpr/reduce_sum | solution.py:55
  300.2 4.5 %bitcast_add_fusion.4 = f32[192,2,8,128]{3,0,2,1:T(8,128)} fusion(f32[192,2,8,128]{3,0,2,1:T(8,128)} %get-tuple-element.252, f32[2,512,192,8]{1,2,3,0:T(8,128)S(1)} %copy-done.1, f32[192,2,8]{0,2,1:T(8,128)S(1)} %select_maximum_fusion.2, pred[192,512]{1,0:T(8,128)(4,1)S(1)} %compare_and_fusion.2, f32[192,2,8]{0,2,1:T(8,128)S(1)} %get-tuple-element.233, ...), kind=kOutput, calls=%fused_computation.14.clone.1 | convolution fusion | flops 410124288 | bytes 9822209 | tf_op jit(solution)/shard_map/while/body/eval_jaxpr/qkgs,skd->qkgd/dot_general | solution.py:57
  307.2 11.3 %all-gather.8.cloned.1.call-done = bf16[2048,1024]{1,0:T(8,128)(2,1)} async-done(((bf16[128,1024]{1,0:T(8,128)(2,1)}), bf16[2048,1024]{1,0:T(8,128)(2,1)}) %all-gather.8.cloned.1.call-update) | async-done | bytes 4194320 | tf_op jit(solution)/shard_map/all_gather | solution.py:82
  322.3 25.8 %all_to_all.10 = bf16[16,24,1024]{2,1,0:T(8,128)(2,1)S(1)} all-to-all(bf16[16,24,1024]{2,1,0:T(8,128)(2,1)S(1)} %bitcast.127), channel_id=1, replica_groups=mesh['ctx'=16,'exp'=16,'dp'=2] {'exp'}, dimensions={0} | all-to-all | bytes 1572864 | tf_op jit(solution)/shard_map/all_to_all | solution.py:112
  355.9 20.9 %all-to-all-done.1 = bf16[16,24,1024]{2,1,0:T(8,128)(2,1)S(1)} async-done(((bf16[16,24,1024]{2,1,0:T(8,128)(2,1)}), bf16[16,24,1024]{2,1,0:T(8,128)(2,1)S(1)}, u32[]{:S(2)}, u32[]{:S(2)}) %all-to-all-start.1) | async-done | bytes 786464 | tf_op jit(solution)/shard_map/all_to_all | solution.py:121
  376.9 5.8 %gather_fusion = bf16[1536,1024]{1,0:T(8,128)(2,1)} fusion(bf16[385,1024]{1,0:T(8,128)(2,1)S(1)} %concatenate.3, s32[2048]{0:T(1024)S(1)} %pad_clamp_fusion), kind=kCustom, calls=%fused_computation | custom fusion | bytes 6297600 | tf_op jit(solution)/shard_map/gather | solution.py:132
  (133 shorter events, 70.8 us)
Async XLA Ops:
  6.5 342.2 %copy-start = (bf16[1,384,1024]{2,1,0:T(8,128)(2,1)S(1)}, bf16[1,384,1024]{2,1,0:T(8,128)(2,1)}, u32[]{:S(2)}) copy-start(bf16[1,384,1024]{2,1,0:T(8,128)(2,1)} %param.25) | copy-start | bytes 2359300
  6.5 94.1 %all-gather.6.cloned.1.call-start = ((), (), s32[]{:S(2)}) async-start(), calls=%async_computation.3 | async-start | bytes 1671168 | tf_op jit(solution)/shard_map/all_gather | solution.py:70
  7.3 177.6 %all-gather.4.cloned.1.call-start = ((), (), s32[]{:S(2)}) async-start(), calls=%async_computation.2 | async-start | bytes 1671168 | tf_op jit(solution)/shard_map/all_gather | solution.py:69
  8.0 310.5 %all-gather.8.cloned.1.call-start = ((), (), s32[]{:S(2)}) async-start(), calls=%async_computation.4 | async-start | bytes 4456448 | tf_op jit(solution)/shard_map/all_gather | solution.py:82
  9.6 9.6 %copy-start.2 = (s32[1,192,8]{2,1,0:T(8,128)}, s32[1,192,8]{2,1,0:T(8,128)S(1)}, u32[]{:S(2)}) copy-start(s32[1,192,8]{2,1,0:T(8,128)S(1)} %copy.27) | copy-start | bytes 18436
  15.7 0.6 copy-start.6
  198.7 4.9 %copy-start.1 = (f32[2,512,192,8]{1,2,3,0:T(8,128)S(1)}, f32[2,512,192,8]{1,2,3,0:T(8,128)}, u32[]{:S(2)}) copy-start(f32[2,512,192,8]{1,2,3,0:T(8,128)} %get-tuple-element.231) | copy-start | bytes 18874372 | tf_op jit(solution)/shard_map/while
  217.1 4.7 %copy-start.1 = (f32[2,512,192,8]{1,2,3,0:T(8,128)S(1)}, f32[2,512,192,8]{1,2,3,0:T(8,128)}, u32[]{:S(2)}) copy-start(f32[2,512,192,8]{1,2,3,0:T(8,128)} %get-tuple-element.231) | copy-start | bytes 18874372 | tf_op jit(solution)/shard_map/while
  236.7 4.6 %copy-start.1 = (f32[2,512,192,8]{1,2,3,0:T(8,128)S(1)}, f32[2,512,192,8]{1,2,3,0:T(8,128)}, u32[]{:S(2)}) copy-start(f32[2,512,192,8]{1,2,3,0:T(8,128)} %get-tuple-element.231) | copy-start | bytes 18874372 | tf_op jit(solution)/shard_map/while
  256.4 4.6 %copy-start.1 = (f32[2,512,192,8]{1,2,3,0:T(8,128)S(1)}, f32[2,512,192,8]{1,2,3,0:T(8,128)}, u32[]{:S(2)}) copy-start(f32[2,512,192,8]{1,2,3,0:T(8,128)} %get-tuple-element.231) | copy-start | bytes 18874372 | tf_op jit(solution)/shard_map/while
  275.9 4.7 %copy-start.1 = (f32[2,512,192,8]{1,2,3,0:T(8,128)S(1)}, f32[2,512,192,8]{1,2,3,0:T(8,128)}, u32[]{:S(2)}) copy-start(f32[2,512,192,8]{1,2,3,0:T(8,128)} %get-tuple-element.231) | copy-start | bytes 18874372 | tf_op jit(solution)/shard_map/while
  295.6 4.6 %copy-start.1 = (f32[2,512,192,8]{1,2,3,0:T(8,128)S(1)}, f32[2,512,192,8]{1,2,3,0:T(8,128)}, u32[]{:S(2)}) copy-start(f32[2,512,192,8]{1,2,3,0:T(8,128)} %get-tuple-element.231) | copy-start | bytes 18874372 | tf_op jit(solution)/shard_map/while
  304.8 13.8 %copy-start.10 = (bf16[1,192,1024]{2,1,0:T(8,128)(2,1)S(1)}, bf16[1,192,1024]{2,1,0:T(8,128)(2,1)}, u32[]{:S(2)}) copy-start(bf16[1,192,1024]{2,1,0:T(8,128)(2,1)} %param.18) | copy-start | bytes 1179652
  318.5 3.3 copy-start.5
  318.5 3.3 copy-start.9
  321.8 26.3 %copy-start.4 = (bf16[1,1024,384]{2,1,0:T(8,128)(2,1)S(1)}, bf16[1,1024,384]{2,1,0:T(8,128)(2,1)}, u32[]{:S(2)}) copy-start(bf16[1,1024,384]{2,1,0:T(8,128)(2,1)} %param.23) | copy-start | bytes 2359300
  348.7 6.7 %copy-start.7 = (s32[1536]{0:T(1024)S(1)}, s32[1536]{0:T(1024)}, u32[]{:S(2)}) copy-start(s32[1536]{0:T(1024)} %copy-done.6) | copy-start | bytes 18436
  348.7 6.9 %copy-start.3 = (s32[1,192,8]{2,1,0:T(8,128)S(1)}, s32[1,192,8]{2,1,0:T(8,128)}, u32[]{:S(2)}) copy-start(s32[1,192,8]{2,1,0:T(8,128)} %copy-done.2) | copy-start | bytes 18436
  348.7 7.0 %copy-start.8 = (f32[1,192,8]{1,2,0:T(8,128)S(1)}, f32[1,192,8]{1,2,0:T(8,128)}, u32[]{:S(2)}) copy-start(f32[1,192,8]{1,2,0:T(8,128)} %param.22) | copy-start | bytes 18436
  351.8 25.0 %all-to-all-start.1 = ((bf16[16,24,1024]{2,1,0:T(8,128)(2,1)}), bf16[16,24,1024]{2,1,0:T(8,128)(2,1)S(1)}, u32[]{:S(2)}, u32[]{:S(2)}) async-start(bf16[16,24,1024]{2,1,0:T(8,128)(2,1)} %bitcast.13), calls=%async_computation.1 | async-start | bytes 1572864 | tf_op jit(solution)/shard_map/all_to_all | solution.py:121
Sparse Core Ops, SparseCore 0:
  10.4 90.1 all-gather.5
  103.7 81.1 all-gather.3
  187.9 130.5 all-gather.7
where the time goes:
time: 395 us; the launch traced here: 393 us
  waiting for transfers between devices  196 us (50%)
  matrix products  58.6 us (15%)
  other arithmetic  44.6 us (11%)
  local copies, waits for them, and re-layouts  39.7 us (10%)
  blocking collectives  25.8 us (7%)
  between operations  13.4 us (3%)
  loops' own time  11.2 us (3%)
    all_gather x1, waiting for transfers between devices, per_device(): key_piece = lax.all_gather(keys, 'ctx', axis=1, tiled=True)  81.9 us
    all_gather x1, waiting for transfers between devices, per_device(): value_piece = lax.all_gather(values, 'ctx', axis=1, tiled=True)  79.8 us
    reduce_sum x6, other arithmetic, attend_block(): new_sum = run_sum * correction + jnp.sum(expo, axis=-1)  26 us
    dot_general x6, matrix products, attend_block(): jnp.einsum('qkgs,skd->qkgd', probs, value_blk, preferred_element_type=jnp...  25.9 us
    all_to_all x1, blocking collectives, per_device(): lax.all_to_all(outgoing, 'exp', split_axis=0, concat_axis=0, tiled=True)  25.8 us
    dot_general x6, matrix products, attend_block(): jnp.einsum('qkgd,skd->qkgs', query_heads, key_blk, preferred_element_type...  22.4 us
    all_to_all x1, waiting for transfers between devices, per_device(): lax.all_to_all(expert_out.reshape(owners, item_count, model_width), 'exp'...  20.9 us
    dynamic_slice x12, local copies, waits for them, and re-layouts, per_device(): lax.scan(attend_block, running, (key_blocks, value_blocks, blk_starts))  15.4 us
  transfers between devices with their start and end apart: 4, of which 4 were waited for; matrix products, arithmetic and copies ran while one was open for 31% of the time, Pallas kernels for 0%

commit v1 on v0

--- a/solution.py
+++ b/solution.py
@@ -67,7 +67,10 @@
     )
     running = initial
     key_piece = lax.all_gather(keys, "ctx", axis=1, tiled=True)
-    value_piece = lax.all_gather(values, "ctx", axis=1, tiled=True)
+    size = lax.axis_size("ctx")
+    blocks = jnp.stack([values for _ in range(size)])
+    blocks = lax.all_to_all(blocks, "ctx", split_axis=0, concat_axis=0)
+    value_piece = jnp.concatenate(blocks, axis=1)
     row_count = key_piece.shape[1]
     blk_rows = math.gcd(row_count, 512)
     blk_count = row_count // blk_rows

time: 395 us -> 365 us (0.924)
  waiting for transfers between devices: 196 us -> 159 us
  starting transfers between devices: 3.69 us -> 22.1 us
  other arithmetic: 44.6 us -> 39.3 us
    all_gather x1 -> x0, waiting for transfers between devices: 79.8 us -> none  [per_device(): value_piece = lax.all_gather(values, 'ctx', axis=1, tiled=True)]
    all_gather x1, waiting for transfers between devices: 81.9 us -> 118 us  [per_device(): key_piece = lax.all_gather(keys, 'ctx', axis=1, tiled=True)]
    all_to_all x0 -> x1, starting transfers between devices: none -> 18.4 us  [per_device(): blocks = lax.all_to_all(blocks, 'ctx', split_axis=0, concat_axis=0)]
    all_gather x1, waiting for transfers between devices: 11.3 us -> 18.7 us  [per_device(): lax.all_gather(out_weight, 'ctx', axis=0, tiled=True)]
    and x6, other arithmetic: 4.96 us -> 0.89 us  [attend_block(): (key_pos[None, :] <= query_pos[:, None]) & (key_seg[None, :] == query_seg...]
  transfers between devices with their start and end apart: 4 -> 4, of which waited for: 4 -> 3; matrix products, arithmetic and copies ran while one was open for 31% -> 31% of each run, Pallas kernels for 0% -> 0%
where the time goes in v1:
time: 365 us; the launch traced here: 364 us
  waiting for transfers between devices  159 us (44%)
  matrix products  58.4 us (16%)
  other arithmetic  39.3 us (11%)
  local copies, waits for them, and re-layouts  35.9 us (10%)
  blocking collectives  25.7 us (7%)
  starting transfers between devices  22.1 us (6%)
  between operations  13.7 us (4%)
  loops' own time  10.3 us (3%)
    all_gather x1, waiting for transfers between devices, per_device(): key_piece = lax.all_gather(keys, 'ctx', axis=1, tiled=True)  118 us
    reduce_sum x6, other arithmetic, attend_block(): new_sum = run_sum * correction + jnp.sum(expo, axis=-1)  26.3 us
    all_to_all x1, blocking collectives, per_device(): lax.all_to_all(outgoing, 'exp', split_axis=0, concat_axis=0, tiled=True)  25.7 us
    dot_general x6, matrix products, attend_block(): jnp.einsum('qkgs,skd->qkgd', probs, value_blk, preferred_element_type=jnp...  25.6 us
    dot_general x6, matrix products, attend_block(): jnp.einsum('qkgd,skd->qkgs', query_heads, key_blk, preferred_element_type...  22.5 us
    all_to_all x1, waiting for transfers between devices, per_device(): lax.all_to_all(expert_out.reshape(owners, item_count, model_width), 'exp'...  20.9 us
    all_gather x1, waiting for transfers between devices, per_device(): lax.all_gather(out_weight, 'ctx', axis=0, tiled=True)  18.7 us
    all_to_all x1, starting transfers between devices, per_device(): blocks = lax.all_to_all(blocks, 'ctx', split_axis=0, concat_axis=0)  18.4 us
  transfers between devices with their start and end apart: 4, of which 3 were waited for; matrix products, arithmetic and copies ran while one was open for 31% of the time, Pallas kernels for 0%

profile of v1, /device:TPU:1, one launch (start us, length us, event | category | flops | bytes accessed | tf_op | source)
XLA Modules:
  0.0 364.0 jit_solution(7091263549598697016)
XLA Ops:
  8.9 18.4 %all-to-all-start = ((bf16[16,1,192,256]{3,2,1,0:T(8,128)(2,1)}), bf16[16,1,192,256]{3,2,1,0:T(8,128)(2,1)S(1)}, u32[]{:S(2)}, u32[]{:S(2)}) async-start(bf16[16,1,192,256]{3,2,1,0:T(8,128)(2,1)} %stack.2), calls=%async_computation | async-start | bytes 3145728 | tf_op jit(solution)/shard_map/all_to_all | solution.py:72
  29.2 4.5 %reduce-window.6 = s32[16,12,128]{2,1,0:T(8,128)S(1)} reduce-window(s32[16,12,128]{2,1,0:T(8,128)S(1)} %fusion.41, s32[]{:T(128)} %constant.11.clone.1), window={size=1x1x128 pad=0_0x0_0x127_0}, to_apply=%region_4.5 | reduce-window | flops 3121152 | bytes 196612 | tf_op jit(solution)/shard_map/reduce-window
  37.7 117.6 %all-gather.3.cloned.1.call-done = bf16[1,3072,256]{2,1,0:T(8,128)(2,1)} async-done(((bf16[1,192,256]{2,1,0:T(8,128)(2,1)}), bf16[1,3072,256]{2,1,0:T(8,128)(2,1)}) %all-gather.3.cloned.1.call-update) | async-done | bytes 1572880 | tf_op jit(solution)/shard_map/all_gather | solution.py:69
  160.7 107.5 %while.15 = (s32[]{:T(128)}, f32[192,2,8]{0,2,1:T(8,128)S(1)}, f32[192,2,8]{0,2,1:T(8,128)S(1)}, f32[192,2,8,128]{3,0,2,1:T(8,128)}, s32[6]{0:T(128)S(1)}, /*ind...) while((s32[]{:T(128)}, f32[192,2,8]{0,2,1:T(8,128)S(1)}, ...), condition=%wide.region_3.4_spmd.clone, body=%wide.region_0.3_spmd.clone.sunk | while | flops 824098496 | bytes 50147816 | solution.py:80
  165.9 3.8 %fusion.60 = (f32[192,2,8]{0,2,1:T(8,128)S(1)}, f32[2,512,192,8]{1,2,3,0:T(8,128)}) fusion(pred[192,512]{1,0:T(8,128)(4,1)S(1)} %compare_and_fusion.2, bf16[192,2,8,128]{3,0,2,1:T(8,128)(2,1)S(1)} %get-tuple-element.282, bf16[1,512,2,128]{3,2,1,0:T(2,128)(2,1)S(1)} %get-tuple-element.240), kind=kOutput, calls=%fused_computation.4.clone.1 | convolution fusion | flops 407368704 | bytes 7450624 | tf_op jit(solution)/shard_map/while/body/eval_jaxpr/qkgd,skd->qkgs/dot_general | solution.py:45
  169.6 4.4 %fusion.61 = f32[192,2,8]{0,2,1:T(8,128)S(1)} fusion(f32[2,512,192,8]{1,2,3,0:T(8,128)} %get-tuple-element.242, f32[192,2,8]{0,2,1:T(8,128)S(1)} %select_maximum_fusion.2, pred[192,512]{1,0:T(8,128)(4,1)S(1)} %compare_and_fusion.2), kind=kLoop, calls=%fused_computation.8.clone.1 | loop fusion | flops 6288384 | bytes 6414336 | tf_op jit(solution)/shard_map/while/body/eval_jaxpr/reduce_sum | solution.py:55
  182.8 3.7 %fusion.60 = (f32[192,2,8]{0,2,1:T(8,128)S(1)}, f32[2,512,192,8]{1,2,3,0:T(8,128)}) fusion(pred[192,512]{1,0:T(8,128)(4,1)S(1)} %compare_and_fusion.2, bf16[192,2,8,128]{3,0,2,1:T(8,128)(2,1)S(1)} %get-tuple-element.282, bf16[1,512,2,128]{3,2,1,0:T(2,128)(2,1)S(1)} %get-tuple-element.240), kind=kOutput, calls=%fused_computation.4.clone.1 | convolution fusion | flops 407368704 | bytes 7450624 | tf_op jit(solution)/shard_map/while/body/eval_jaxpr/qkgd,skd->qkgs/dot_general | solution.py:45
  186.5 4.4 %fusion.61 = f32[192,2,8]{0,2,1:T(8,128)S(1)} fusion(f32[2,512,192,8]{1,2,3,0:T(8,128)} %get-tuple-element.242, f32[192,2,8]{0,2,1:T(8,128)S(1)} %select_maximum_fusion.2, pred[192,512]{1,0:T(8,128)(4,1)S(1)} %compare_and_fusion.2), kind=kLoop, calls=%fused_computation.8.clone.1 | loop fusion | flops 6288384 | bytes 6414336 | tf_op jit(solution)/shard_map/while/body/eval_jaxpr/reduce_sum | solution.py:55
  191.2 4.5 %bitcast_add_fusion.4 = f32[192,2,8,128]{3,0,2,1:T(8,128)} fusion(f32[192,2,8,128]{3,0,2,1:T(8,128)} %get-tuple-element.263, f32[2,512,192,8]{1,2,3,0:T(8,128)S(1)} %copy-done.1, f32[192,2,8]{0,2,1:T(8,128)S(1)} %select_maximum_fusion.2, pred[192,512]{1,0:T(8,128)(4,1)S(1)} %compare_and_fusion.2, f32[192,2,8]{0,2,1:T(8,128)S(1)} %get-tuple-element.244, ...), kind=kOutput, calls=%fused_computation.14.clone.1 | convolution fusion | flops 410124288 | bytes 9822209 | tf_op jit(solution)/shard_map/while/body/eval_jaxpr/qkgs,skd->qkgd/dot_general | solution.py:57
  204.6 4.4 %fusion.61 = f32[192,2,8]{0,2,1:T(8,128)S(1)} fusion(f32[2,512,192,8]{1,2,3,0:T(8,128)} %get-tuple-element.242, f32[192,2,8]{0,2,1:T(8,128)S(1)} %select_maximum_fusion.2, pred[192,512]{1,0:T(8,128)(4,1)S(1)} %compare_and_fusion.2), kind=kLoop, calls=%fused_computation.8.clone.1 | loop fusion | flops 6288384 | bytes 6414336 | tf_op jit(solution)/shard_map/while/body/eval_jaxpr/reduce_sum | solution.py:55
  209.3 4.5 %bitcast_add_fusion.4 = f32[192,2,8,128]{3,0,2,1:T(8,128)} fusion(f32[192,2,8,128]{3,0,2,1:T(8,128)} %get-tuple-element.263, f32[2,512,192,8]{1,2,3,0:T(8,128)S(1)} %copy-done.1, f32[192,2,8]{0,2,1:T(8,128)S(1)} %select_maximum_fusion.2, pred[192,512]{1,0:T(8,128)(4,1)S(1)} %compare_and_fusion.2, f32[192,2,8]{0,2,1:T(8,128)S(1)} %get-tuple-element.244, ...), kind=kOutput, calls=%fused_computation.14.clone.1 | convolution fusion | flops 410124288 | bytes 9822209 | tf_op jit(solution)/shard_map/while/body/eval_jaxpr/qkgs,skd->qkgd/dot_general | solution.py:57
  219.0 3.8 %fusion.60 = (f32[192,2,8]{0,2,1:T(8,128)S(1)}, f32[2,512,192,8]{1,2,3,0:T(8,128)}) fusion(pred[192,512]{1,0:T(8,128)(4,1)S(1)} %compare_and_fusion.2, bf16[192,2,8,128]{3,0,2,1:T(8,128)(2,1)S(1)} %get-tuple-element.282, bf16[1,512,2,128]{3,2,1,0:T(2,128)(2,1)S(1)} %get-tuple-element.240), kind=kOutput, calls=%fused_computation.4.clone.1 | convolution fusion | flops 407368704 | bytes 7450624 | tf_op jit(solution)/shard_map/while/body/eval_jaxpr/qkgd,skd->qkgs/dot_general | solution.py:45
  222.7 4.4 %fusion.61 = f32[192,2,8]{0,2,1:T(8,128)S(1)} fusion(f32[2,512,192,8]{1,2,3,0:T(8,128)} %get-tuple-element.242, f32[192,2,8]{0,2,1:T(8,128)S(1)} %select_maximum_fusion.2, pred[192,512]{1,0:T(8,128)(4,1)S(1)} %compare_and_fusion.2), kind=kLoop, calls=%fused_computation.8.clone.1 | loop fusion | flops 6288384 | bytes 6414336 | tf_op jit(solution)/shard_map/while/body/eval_jaxpr/reduce_sum | solution.py:55
  227.4 4.5 %bitcast_add_fusion.4 = f32[192,2,8,128]{3,0,2,1:T(8,128)} fusion(f32[192,2,8,128]{3,0,2,1:T(8,128)} %get-tuple-element.263, f32[2,512,192,8]{1,2,3,0:T(8,128)S(1)} %copy-done.1, f32[192,2,8]{0,2,1:T(8,128)S(1)} %select_maximum_fusion.2, pred[192,512]{1,0:T(8,128)(4,1)S(1)} %compare_and_fusion.2, f32[192,2,8]{0,2,1:T(8,128)S(1)} %get-tuple-element.244, ...), kind=kOutput, calls=%fused_computation.14.clone.1 | convolution fusion | flops 410124288 | bytes 9822209 | tf_op jit(solution)/shard_map/while/body/eval_jaxpr/qkgs,skd->qkgd/dot_general | solution.py:57
  237.1 3.8 %fusion.60 = (f32[192,2,8]{0,2,1:T(8,128)S(1)}, f32[2,512,192,8]{1,2,3,0:T(8,128)}) fusion(pred[192,512]{1,0:T(8,128)(4,1)S(1)} %compare_and_fusion.2, bf16[192,2,8,128]{3,0,2,1:T(8,128)(2,1)S(1)} %get-tuple-element.282, bf16[1,512,2,128]{3,2,1,0:T(2,128)(2,1)S(1)} %get-tuple-element.240), kind=kOutput, calls=%fused_computation.4.clone.1 | convolution fusion | flops 407368704 | bytes 7450624 | tf_op jit(solution)/shard_map/while/body/eval_jaxpr/qkgd,skd->qkgs/dot_general | solution.py:45
  240.8 4.4 %fusion.61 = f32[192,2,8]{0,2,1:T(8,128)S(1)} fusion(f32[2,512,192,8]{1,2,3,0:T(8,128)} %get-tuple-element.242, f32[192,2,8]{0,2,1:T(8,128)S(1)} %select_maximum_fusion.2, pred[192,512]{1,0:T(8,128)(4,1)S(1)} %compare_and_fusion.2), kind=kLoop, calls=%fused_computation.8.clone.1 | loop fusion | flops 6288384 | bytes 6414336 | tf_op jit(solution)/shard_map/while/body/eval_jaxpr/reduce_sum | solution.py:55
  245.4 4.5 %bitcast_add_fusion.4 = f32[192,2,8,128]{3,0,2,1:T(8,128)} fusion(f32[192,2,8,128]{3,0,2,1:T(8,128)} %get-tuple-element.263, f32[2,512,192,8]{1,2,3,0:T(8,128)S(1)} %copy-done.1, f32[192,2,8]{0,2,1:T(8,128)S(1)} %select_maximum_fusion.2, pred[192,512]{1,0:T(8,128)(4,1)S(1)} %compare_and_fusion.2, f32[192,2,8]{0,2,1:T(8,128)S(1)} %get-tuple-element.244, ...), kind=kOutput, calls=%fused_computation.14.clone.1 | convolution fusion | flops 410124288 | bytes 9822209 | tf_op jit(solution)/shard_map/while/body/eval_jaxpr/qkgs,skd->qkgd/dot_general | solution.py:57
  255.1 3.7 %fusion.60 = (f32[192,2,8]{0,2,1:T(8,128)S(1)}, f32[2,512,192,8]{1,2,3,0:T(8,128)}) fusion(pred[192,512]{1,0:T(8,128)(4,1)S(1)} %compare_and_fusion.2, bf16[192,2,8,128]{3,0,2,1:T(8,128)(2,1)S(1)} %get-tuple-element.282, bf16[1,512,2,128]{3,2,1,0:T(2,128)(2,1)S(1)} %get-tuple-element.240), kind=kOutput, calls=%fused_computation.4.clone.1 | convolution fusion | flops 407368704 | bytes 7450624 | tf_op jit(solution)/shard_map/while/body/eval_jaxpr/qkgd,skd->qkgs/dot_general | solution.py:45
  258.9 4.4 %fusion.61 = f32[192,2,8]{0,2,1:T(8,128)S(1)} fusion(f32[2,512,192,8]{1,2,3,0:T(8,128)} %get-tuple-element.242, f32[192,2,8]{0,2,1:T(8,128)S(1)} %select_maximum_fusion.2, pred[192,512]{1,0:T(8,128)(4,1)S(1)} %compare_and_fusion.2), kind=kLoop, calls=%fused_computation.8.clone.1 | loop fusion | flops 6288384 | bytes 6414336 | tf_op jit(solution)/shard_map/while/body/eval_jaxpr/reduce_sum | solution.py:55
  263.6 4.5 %bitcast_add_fusion.4 = f32[192,2,8,128]{3,0,2,1:T(8,128)} fusion(f32[192,2,8,128]{3,0,2,1:T(8,128)} %get-tuple-element.263, f32[2,512,192,8]{1,2,3,0:T(8,128)S(1)} %copy-done.1, f32[192,2,8]{0,2,1:T(8,128)S(1)} %select_maximum_fusion.2, pred[192,512]{1,0:T(8,128)(4,1)S(1)} %compare_and_fusion.2, f32[192,2,8]{0,2,1:T(8,128)S(1)} %get-tuple-element.244, ...), kind=kOutput, calls=%fused_computation.14.clone.1 | convolution fusion | flops 410124288 | bytes 9822209 | tf_op jit(solution)/shard_map/while/body/eval_jaxpr/qkgs,skd->qkgd/dot_general | solution.py:57
  270.7 18.7 %all-gather.5.cloned.1.call-done = bf16[2048,1024]{1,0:T(8,128)(2,1)} async-done(((bf16[128,1024]{1,0:T(8,128)(2,1)}), bf16[2048,1024]{1,0:T(8,128)(2,1)}) %all-gather.5.cloned.1.call-update) | async-done | bytes 4194320 | tf_op jit(solution)/shard_map/all_gather | solution.py:85
  293.1 25.7 %all_to_all.15 = bf16[16,24,1024]{2,1,0:T(8,128)(2,1)S(1)} all-to-all(bf16[16,24,1024]{2,1,0:T(8,128)(2,1)S(1)} %bitcast.130), channel_id=1, replica_groups=mesh['ctx'=16,'exp'=16,'dp'=2] {'exp'}, dimensions={0} | all-to-all | bytes 1572864 | tf_op jit(solution)/shard_map/all_to_all | solution.py:115
  326.5 20.9 %all-to-all-done.2 = bf16[16,24,1024]{2,1,0:T(8,128)(2,1)S(1)} async-done(((bf16[16,24,1024]{2,1,0:T(8,128)(2,1)}), bf16[16,24,1024]{2,1,0:T(8,128)(2,1)S(1)}, u32[]{:S(2)}, u32[]{:S(2)}) %all-to-all-start.2) | async-done | bytes 786464 | tf_op jit(solution)/shard_map/all_to_all | solution.py:124
  347.5 5.8 %gather_fusion = bf16[1536,1024]{1,0:T(8,128)(2,1)} fusion(bf16[385,1024]{1,0:T(8,128)(2,1)S(1)} %concatenate.3, s32[2048]{0:T(1024)S(1)} %pad_clamp_fusion), kind=kCustom, calls=%fused_computation | custom fusion | bytes 6297600 | tf_op jit(solution)/shard_map/gather | solution.py:135
  (129 shorter events, 60.7 us)
Async XLA Ops:
  6.5 312.9 %copy-start = (bf16[1,384,1024]{2,1,0:T(8,128)(2,1)S(1)}, bf16[1,384,1024]{2,1,0:T(8,128)(2,1)}, u32[]{:S(2)}) copy-start(bf16[1,384,1024]{2,1,0:T(8,128)(2,1)} %param.25) | copy-start | bytes 2359300
  6.5 22.2 %copy-start.5 = (s32[1,192,8]{1,2,0:T(8,128)S(1)}, s32[1,192,8]{1,2,0:T(8,128)}, u32[]{:S(2)}) copy-start(s32[1,192,8]{1,2,0:T(8,128)} %param.21) | copy-start | bytes 18436
  8.9 149.9 %all-to-all-start = ((bf16[16,1,192,256]{3,2,1,0:T(8,128)(2,1)}), bf16[16,1,192,256]{3,2,1,0:T(8,128)(2,1)S(1)}, u32[]{:S(2)}, u32[]{:S(2)}) async-start(bf16[16,1,192,256]{3,2,1,0:T(8,128)(2,1)} %stack.2), calls=%async_computation | async-start | bytes 3145728 | tf_op jit(solution)/shard_map/all_to_all | solution.py:72
  27.3 128.0 %all-gather.3.cloned.1.call-start = ((), (), s32[]{:S(2)}) async-start(), calls=%async_computation.3 | async-start | bytes 1671168 | tf_op jit(solution)/shard_map/all_gather | solution.py:69
  28.0 261.3 %all-gather.5.cloned.1.call-start = ((), (), s32[]{:S(2)}) async-start(), calls=%async_computation.4 | async-start | bytes 4456448 | tf_op jit(solution)/shard_map/all_gather | solution.py:85
  169.6 4.9 %copy-start.1 = (f32[2,512,192,8]{1,2,3,0:T(8,128)S(1)}, f32[2,512,192,8]{1,2,3,0:T(8,128)}, u32[]{:S(2)}) copy-start(f32[2,512,192,8]{1,2,3,0:T(8,128)} %get-tuple-element.242) | copy-start | bytes 18874372 | tf_op jit(solution)/shard_map/while
  186.5 4.7 %copy-start.1 = (f32[2,512,192,8]{1,2,3,0:T(8,128)S(1)}, f32[2,512,192,8]{1,2,3,0:T(8,128)}, u32[]{:S(2)}) copy-start(f32[2,512,192,8]{1,2,3,0:T(8,128)} %get-tuple-element.242) | copy-start | bytes 18874372 | tf_op jit(solution)/shard_map/while
  204.6 4.6 %copy-start.1 = (f32[2,512,192,8]{1,2,3,0:T(8,128)S(1)}, f32[2,512,192,8]{1,2,3,0:T(8,128)}, u32[]{:S(2)}) copy-start(f32[2,512,192,8]{1,2,3,0:T(8,128)} %get-tuple-element.242) | copy-start | bytes 18874372 | tf_op jit(solution)/shard_map/while
  222.7 4.7 %copy-start.1 = (f32[2,512,192,8]{1,2,3,0:T(8,128)S(1)}, f32[2,512,192,8]{1,2,3,0:T(8,128)}, u32[]{:S(2)}) copy-start(f32[2,512,192,8]{1,2,3,0:T(8,128)} %get-tuple-element.242) | copy-start | bytes 18874372 | tf_op jit(solution)/shard_map/while
  240.8 4.6 %copy-start.1 = (f32[2,512,192,8]{1,2,3,0:T(8,128)S(1)}, f32[2,512,192,8]{1,2,3,0:T(8,128)}, u32[]{:S(2)}) copy-start(f32[2,512,192,8]{1,2,3,0:T(8,128)} %get-tuple-element.242) | copy-start | bytes 18874372 | tf_op jit(solution)/shard_map/while
  258.9 4.8 %copy-start.1 = (f32[2,512,192,8]{1,2,3,0:T(8,128)S(1)}, f32[2,512,192,8]{1,2,3,0:T(8,128)}, u32[]{:S(2)}) copy-start(f32[2,512,192,8]{1,2,3,0:T(8,128)} %get-tuple-element.242) | copy-start | bytes 18874372 | tf_op jit(solution)/shard_map/while
  268.2 21.1 %copy-start.8 = (bf16[1,192,1024]{2,1,0:T(8,128)(2,1)S(1)}, bf16[1,192,1024]{2,1,0:T(8,128)(2,1)}, u32[]{:S(2)}) copy-start(bf16[1,192,1024]{2,1,0:T(8,128)(2,1)} %param.18) | copy-start | bytes 1179652
  289.3 3.3 copy-start.7
  292.6 26.2 %copy-start.2 = (f32[192,1024]{1,0:T(8,128)}, f32[192,1024]{1,0:T(8,128)S(1)}, u32[]{:S(2)}) copy-start(f32[192,1024]{1,0:T(8,128)S(1)} %get-tuple-element.166) | copy-start | bytes 2359300
  292.6 26.2 %copy-start.4 = (bf16[1,1024,384]{2,1,0:T(8,128)(2,1)S(1)}, bf16[1,1024,384]{2,1,0:T(8,128)(2,1)}, u32[]{:S(2)}) copy-start(bf16[1,1024,384]{2,1,0:T(8,128)(2,1)} %param.23) | copy-start | bytes 2359300
  319.4 6.9 %copy-start.6 = (f32[1,192,8]{1,2,0:T(8,128)S(1)}, f32[1,192,8]{1,2,0:T(8,128)}, u32[]{:S(2)}) copy-start(f32[1,192,8]{1,2,0:T(8,128)} %param.22) | copy-start | bytes 18436
  322.5 25.0 %all-to-all-start.2 = ((bf16[16,24,1024]{2,1,0:T(8,128)(2,1)}), bf16[16,24,1024]{2,1,0:T(8,128)(2,1)S(1)}, u32[]{:S(2)}, u32[]{:S(2)}) async-start(bf16[16,24,1024]{2,1,0:T(8,128)(2,1)} %bitcast.135), calls=%async_computation.2 | async-start | bytes 1572864 | tf_op jit(solution)/shard_map/all_to_all | solution.py:124
  353.3 2.9 copy-start.3
Sparse Core Ops, SparseCore 0:
  31.1 124.1 all-gather.2
  158.3 130.9 all-gather.4
